TPU v7x, 512 devices: a whole 4x8x8 slice. The times are simulated.
512 devices in a mesh: member: 16 (over x, y_lo), lat: 32 (over z, y_hi, core).
Axes of the slice: x: 4, y: 8 (y_hi: 2, y_lo: 4; y = y_hi * 4 + y_lo), z: 8, core: 2. Of those that a mesh axis runs over, the one named last changes fastest.
Arguments:
- states: bfloat16 [16, 64, 256, 256], P('member', 'lat'), may hold values from -6 to 6
- member_id: int32 [16], P('member'), may hold values from 0 to 15, each once
- member_gain: float32 [16, 256], replicated, may hold values from 0.5 to 2
- first_conv: bfloat16 [2304, 256], P('member'), may hold values from -0.125 to 0.125
- second_conv: bfloat16 [2304, 256], P('member'), may hold values from -0.125 to 0.125
- head: bfloat16 [256, 8], replicated, may hold values from -0.375 to 0.375
- target: float32 [8, 64, 256], P(None, 'lat'), may hold values from -6 to 6
- lat_start: int32 [1], replicated, may hold values from 0 to 1737
Outputs:
- score: float32 [8, 64, 256], P(None, 'lat')
- mean_score: float32 [], replicated
All inputs are finite; a program needn't handle non-finite values.
Results may differ from a plain program's by a relative error of at most 0.0018.
Values may be sent and summed in bfloat16 or wider, within the bound.
No kernel may reach another device: no remote copies, remote signals or barrier semaphores. Data moves between devices by JAX's collectives and lax.ppermute only.
A program may use at most 64 MiB of HBM per device.

v0:
```python
import jax
import jax.numpy as jnp
from jax import lax
from jax.sharding import PartitionSpec as P


def with_halo(block, sides, width):
    for axis, dim in sides:
        count = lax.axis_size(axis)
        forward = [(i, i + 1) for i in range(count - 1)]
        backward = [(target, source) for source, target in forward]
        low = lax.ppermute(
            lax.slice_in_dim(block, block.shape[dim] - width, None, axis=dim), axis, forward
        )
        high = lax.ppermute(lax.slice_in_dim(block, 0, width, axis=dim), axis, backward)
        block = jnp.concatenate([low, block, high], axis=dim)
    return block


def product(left, right):
    return jnp.dot(
        left.astype(jnp.float32),
        right.astype(jnp.float32),
        precision=lax.Precision.HIGHEST,
        preferred_element_type=jnp.float32,
    )


def patch_rows(field):
    rows, cols, chans = (field.shape[0] - 2, field.shape[1], field.shape[2])
    padded = jnp.pad(field, ((0, 0), (1, 1), (0, 0)))
    taps = [padded[dy : dy + rows, dx : dx + cols, :] for dy in range(3) for dx in range(3)]
    return jnp.concatenate(taps, axis=-1).reshape(rows * cols, 9 * chans)


def folded_conv(patches, weight_rows):
    return product(patches, lax.all_gather(weight_rows, "member", axis=0, tiled=True))


def body(states, member_id, member_gain, first_conv, second_conv, head, target, lat_start):
    rows, cols, chans = (states.shape[1], states.shape[2], states.shape[3])
    members = lax.axis_size("member")
    band = lax.axis_index("lat")
    select = (jnp.arange(members, dtype=jnp.int32)[None, :] == member_id[:, None]).astype(
        jnp.float32
    )
    gain = jnp.dot(select, member_gain, precision=lax.Precision.HIGHEST)
    start = (states[0].astype(jnp.float32) * gain[0]).astype(jnp.bfloat16)

    def with_rims(field):
        return with_halo(field, (("lat", 0),), 1)

    first_out = folded_conv(patch_rows(with_rims(start)), first_conv)
    inner = jax.nn.gelu(first_out, approximate=True).astype(jnp.bfloat16).reshape(rows, cols, -1)
    second_out = folded_conv(patch_rows(with_rims(inner)), second_conv)
    block = (start.reshape(rows * cols, chans).astype(jnp.float32) + second_out).astype(
        jnp.bfloat16
    )
    pred = product(block, head)
    pred = pred.T.reshape(-1, rows, cols).astype(jnp.bfloat16)
    eps = 0.05 / members
    factor = (1.0 - eps) / (2.0 * members * (members - 1))
    fields = lax.all_gather(pred[None], "member", axis=0, tiled=True).astype(jnp.float32)
    skill = jnp.sum(jnp.abs(fields - target[None]), axis=0) / members

    def pair_step(index, total):
        chosen = lax.dynamic_index_in_dim(fields, index, 0, keepdims=True)
        return total + jnp.sum(jnp.abs(chosen - fields), axis=0)

    spread = lax.fori_loop(0, members, pair_step, jnp.zeros_like(skill))
    score = skill - factor * spread
    row_ids = lat_start[0] + band * rows + jnp.arange(rows, dtype=jnp.int32)
    area = jnp.cos(jnp.pi * (90.0 - 0.1 * row_ids.astype(jnp.float32)) / 180.0)
    weighted, area_total = lax.psum((jnp.sum(score * area[None, :, None]), jnp.sum(area)), "lat")
    mean_score = weighted / (score.shape[0] * cols * area_total)
    return (score, mean_score)


def solution(mesh):
    placed = (
        P("member", "lat", None, None),
        P("member"),
        P(),
        P("member", None),
        P("member", None),
        P(),
        P(None, "lat", None),
        P(),
    )
    return jax.shard_map(
        body, mesh=mesh, in_specs=placed, out_specs=(P(None, "lat", None), P()), check_vma=False
    )
```

profile of v0, /device:TPU:1, one launch (start us, length us, event | category | flops | bytes accessed | tf_op | source)
XLA Modules:
  0.0 331.9 jit_solution(7354187665463545966)
XLA Ops:
  7.2 0.7 all-gather.3.cloned.1.call-update
  8.7 1.0 fusion.15
  9.8 8.8 %collective-permute-start = (bf16[1,256,256]{2,1,0:T(8,128)(2,1)S(1)}, bf16[1,256,256]{2,1,0:T(8,128)(2,1)S(1)}, u32[]{:S(2)}, u32[]{:S(2)}) collective-permute-start(bf16[1,256,256]{2,1,0:T(8,128)(2,1)S(1)} %get-tuple-element.107), channel_id=1, source_target_pairs={{0,1},{1,2},{2,3},{3,4},{4,5},{5,6},{6,7},{7,8},{8,9},{9,10},{10,1... | collective-permute-start | bytes 393224 | tf_op jit(solution)/shard_map/ppermute | solution.py:12
  18.6 1.9 collective-permute-start.1
  20.6 8.2 %collective-permute-done.1 = bf16[1,256,256]{2,1,0:T(8,128)(2,1)S(1)} collective-permute-done((bf16[1,256,256]{2,1,0:T(8,128)(2,1)S(1)}, bf16[1,256,256]{2,1,0:T(8,128)(2,1)S(1)}, u32[]{:S(2)}, u32[]{:S(2)}) %collective-permute-start.1) | collective-permute-done | bytes 131104 | tf_op jit(solution)/shard_map/ppermute | solution.py:15
  29.4 61.0 %all-gather.3.cloned.1.call-done = bf16[2304,256]{1,0:T(8,128)(2,1)} async-done(((bf16[144,256]{1,0:T(8,128)(2,1)}), bf16[2304,256]{1,0:T(8,128)(2,1)}) %all-gather.3.cloned.1.call-update) | async-done | bytes 1179664 | tf_op jit(solution)/shard_map/all_gather | solution.py:37
  90.4 2.1 fusion.14
  92.5 17.7 %collective-permute-start.2 = (bf16[1,256,256]{2,1,0:T(8,128)(2,1)S(1)}, bf16[1,256,256]{2,1,0:T(8,128)(2,1)S(1)}, u32[]{:S(2)}, u32[]{:S(2)}) collective-permute-start(bf16[1,256,256]{2,1,0:T(8,128)(2,1)S(1)} %get-tuple-element.105), channel_id=1, source_target_pairs={{0,1},{1,2},{2,3},{3,4},{4,5},{5,6},{6,7},{7,8},{8,9},{9,10},{10,1... | collective-permute-start | bytes 393224 | tf_op jit(solution)/shard_map/ppermute | solution.py:12
  110.2 1.9 collective-permute-start.3
  112.9 0.7 fusion.25
  113.7 6.8 %collective-permute-done.3 = bf16[1,256,256]{2,1,0:T(8,128)(2,1)S(1)} collective-permute-done((bf16[1,256,256]{2,1,0:T(8,128)(2,1)S(1)}, bf16[1,256,256]{2,1,0:T(8,128)(2,1)S(1)}, u32[]{:S(2)}, u32[]{:S(2)}) %collective-permute-start.3) | collective-permute-done | bytes 131104 | tf_op jit(solution)/shard_map/ppermute | solution.py:15
  120.6 0.2 fusion.27
  120.8 0.8 constant_dynamic-update-slice_fusion.9
  121.7 0.8 constant_dynamic-update-slice_fusion.8
  122.4 0.7 constant_dynamic-update-slice_fusion.7
  123.2 0.7 constant_dynamic-update-slice_fusion.6
  123.9 0.8 constant_dynamic-update-slice_fusion.5
  124.7 0.7 constant_dynamic-update-slice_fusion.4
  125.4 0.7 constant_dynamic-update-slice_fusion.3
  126.1 0.8 constant_dynamic-update-slice_fusion.2
  126.9 0.8 constant_dynamic-update-slice_fusion.1
  127.7 48.5 %all-gather.5.cloned.1.call-done = bf16[2304,256]{1,0:T(8,128)(2,1)} async-done(((bf16[144,256]{1,0:T(8,128)(2,1)}), bf16[2304,256]{1,0:T(8,128)(2,1)}) %all-gather.5.cloned.1.call-update) | async-done | bytes 1179664 | tf_op jit(solution)/shard_map/all_gather | solution.py:37
  176.2 2.8 fusion
  179.0 0.2 convolution_convert_fusion
  179.2 36.0 %all_gather.11 = bf16[16,8,2,256]{3,1,2,0:T(8,128)(2,1)S(1)} all-gather(bf16[1,8,2,256]{3,1,2,0:T(8,128)(2,1)S(1)} %bitcast.56), channel_id=1, replica_groups=mesh['member'=16,'lat'=32] {'member'}, dimensions={0}, use_global_device_ids=true | all-gather | bytes 139264 | tf_op jit(solution)/shard_map/all_gather | solution.py:63
  215.3 3.4 %while.14 = (s32[]{:T(128)}, f32[8,2,256]{2,1,0:T(2,128)S(1)}, f32[16,8,2,256]{3,2,1,0:T(2,128)S(1)}, s32[]{:T(128)}, s32[]{:T(128)}) while((s32[]{:T(128)}, f32[8,2,256]{2,1,0:T(2,128)S(1)}, f32[16,8,2,256]{3,2,1,0:T(2,128)S(1)}, s32[]{:T(128)}, s32[]{:T(128)}) %tuple.48), condition=%wide.region_3.4_spmd.clone, body=%wide.region_1.3_spmd.clone.sunk | while | flops 200707 | bytes 376907 | solution.py:70
  215.3 0.2 abs_reduce_fusion.3
  216.2 0.2 abs_reduce_fusion.3
  216.4 0.2 abs_reduce_fusion.3
  218.8 0.7 multiply_reduce_fusion
  219.5 0.6 copy.16
  220.1 102.5 %all-reduce.2 = (f32[]{:T(128)}, f32[]{:T(128)}) all-reduce(f32[]{:T(128)} %get-tuple-element.95, f32[]{:T(128)} %fusion.25), channel_id=1, replica_groups=mesh['member'=16,'lat'=32] {'lat'}, use_global_device_ids=true, to_apply=%region_5.6 | all-reduce | flops 2 | bytes 16 | tf_op jit(solution)/shard_map/psum | solution.py:74
  (79 shorter events, 3.7 us)
Async XLA Ops:
  7.2 1.5 copy-start
  7.2 21.9 %copy-start.1 = (bf16[1,2,256,256]{3,2,1,0:T(8,128)(2,1)S(1)}, bf16[1,2,256,256]{3,2,1,0:T(8,128)(2,1)}, u32[]{:S(2)}) copy-start(bf16[1,2,256,256]{3,2,1,0:T(8,128)(2,1)} %param.10) | copy-start | bytes 786436
  7.2 83.2 %all-gather.3.cloned.1.call-start = ((), (), s32[]{:S(2)}) async-start(), calls=%async_computation | async-start | bytes 1253376 | tf_op jit(solution)/shard_map/all_gather | solution.py:37
  7.9 168.3 %all-gather.5.cloned.1.call-start = ((), (), s32[]{:S(2)}) async-start(), calls=%async_computation.1 | async-start | bytes 1253376 | tf_op jit(solution)/shard_map/all_gather | solution.py:37
  9.8 10.8 %collective-permute-start = (bf16[1,256,256]{2,1,0:T(8,128)(2,1)S(1)}, bf16[1,256,256]{2,1,0:T(8,128)(2,1)S(1)}, u32[]{:S(2)}, u32[]{:S(2)}) collective-permute-start(bf16[1,256,256]{2,1,0:T(8,128)(2,1)S(1)} %get-tuple-element.107), channel_id=1, source_target_pairs={{0,1},{1,2},{2,3},{3,4},{4,5},{5,6},{6,7},{7,8},{8,9},{9,10},{10,1... | collective-permute-start | bytes 393224 | tf_op jit(solution)/shard_map/ppermute | solution.py:12
  18.6 10.2 %collective-permute-start.1 = (bf16[1,256,256]{2,1,0:T(8,128)(2,1)S(1)}, bf16[1,256,256]{2,1,0:T(8,128)(2,1)S(1)}, u32[]{:S(2)}, u32[]{:S(2)}) collective-permute-start(bf16[1,256,256]{2,1,0:T(8,128)(2,1)S(1)} %get-tuple-element.108), channel_id=1, source_target_pairs={{1,0},{2,1},{3,2},{4,3},{5,4},{6,5},{7,6},{8,7},{9,8},{10,9},{11,1... | collective-permute-start | bytes 393224 | tf_op jit(solution)/shard_map/ppermute | solution.py:15
  90.4 21.8 %copy-start.2 = (f32[8,2,256]{2,1,0:T(2,128)S(1)}, f32[8,2,256]{2,1,0:T(2,128)}, u32[]{:S(2)}) copy-start(f32[8,2,256]{2,1,0:T(2,128)} %param.16) | copy-start | bytes 49156
  92.5 21.1 %collective-permute-start.2 = (bf16[1,256,256]{2,1,0:T(8,128)(2,1)S(1)}, bf16[1,256,256]{2,1,0:T(8,128)(2,1)S(1)}, u32[]{:S(2)}, u32[]{:S(2)}) collective-permute-start(bf16[1,256,256]{2,1,0:T(8,128)(2,1)S(1)} %get-tuple-element.105), channel_id=1, source_target_pairs={{0,1},{1,2},{2,3},{3,4},{4,5},{5,6},{6,7},{7,8},{8,9},{9,10},{10,1... | collective-permute-start | bytes 393224 | tf_op jit(solution)/shard_map/ppermute | solution.py:12
  110.2 10.3 %collective-permute-start.3 = (bf16[1,256,256]{2,1,0:T(8,128)(2,1)S(1)}, bf16[1,256,256]{2,1,0:T(8,128)(2,1)S(1)}, u32[]{:S(2)}, u32[]{:S(2)}) collective-permute-start(bf16[1,256,256]{2,1,0:T(8,128)(2,1)S(1)} %get-tuple-element.106), channel_id=1, source_target_pairs={{1,0},{2,1},{3,2},{4,3},{5,4},{6,5},{7,6},{8,7},{9,8},{10,9},{11,1... | collective-permute-start | bytes 393224 | tf_op jit(solution)/shard_map/ppermute | solution.py:15
  127.7 51.3 %copy-start.3 = (bf16[256,8]{0,1:T(8,128)(2,1)S(1)}, bf16[256,8]{0,1:T(8,128)(2,1)}, u32[]{:S(2)}) copy-start(bf16[256,8]{0,1:T(8,128)(2,1)} %param.15) | copy-start | bytes 12292
Sparse Core Ops, SparseCore 0:
  10.1 80.2 all-gather.2
  92.5 83.7 all-gather.4
where the time goes:
time: 332 us
  blocking collectives  139 us (42%)
  waiting for transfers between devices  125 us (38%)
  starting transfers between devices  30.4 us (9%)
  between operations  18.1 us (5%)
  local copies, waits for them, and re-layouts  8.13 us (2%)
  other arithmetic  5.8 us (2%)
  matrix products  5.15 us (2%)
    all_gather x2, waiting for transfers between devices, folded_conv(): lax.all_gather(weight_rows, 'member', axis=0, tiled=True)  110 us
    psum x1, blocking collectives, body(): lax.psum((jnp.sum(score * area[None, :, None]), jnp.sum(area)), 'lat')  102 us
    all_gather x1, blocking collectives, body(): lax.all_gather(pred[None], 'member', axis=0, tiled=True).astype(jnp.float32)  36 us
    ppermute x2, starting transfers between devices, with_halo(): lax.ppermute(lax.slice_in_dim(block, block.shape[dim] - width, None, axis...  26.5 us
    ppermute x2, waiting for transfers between devices, with_halo(): lax.ppermute(lax.slice_in_dim(block, 0, width, axis=dim), axis, backward)  15.1 us
    unnamed x24, local copies, waits for them, and re-layouts  6.93 us
  transfers between devices with their start and end apart: 6, of which 4 were waited for; matrix products, arithmetic and copies ran while one was open for 4% of the time, Pallas kernels for 0%

commit v1 on v0

--- a/solution.py
+++ b/solution.py
@@ -34,7 +34,13 @@
 
 
 def folded_conv(patches, weight_rows):
-    return product(patches, lax.all_gather(weight_rows, "member", axis=0, tiled=True))
+    return product(
+        patches,
+        jnp.concatenate(
+            lax.all_to_all(jnp.stack([weight_rows] * lax.axis_size("member")), "member", 0, 0),
+            axis=0,
+        ),
+    )
 
 
 def body(states, member_id, member_gain, first_conv, second_conv, head, target, lat_start):

time: 332 us -> 229 us (0.69)
  waiting for transfers between devices: 125 us -> 35.5 us
  between operations: 18.1 us -> 4.5 us
  local copies, waits for them, and re-layouts: 8.13 us -> 15.7 us
  blocking collectives: 139 us -> 132 us
    all_gather x2 -> x0, waiting for transfers between devices: 110 us -> none  [folded_conv(): lax.all_gather(weight_rows, 'member', axis=0, tiled=True)]
    ppermute x2, waiting for transfers between devices: 0.01 us -> 22.3 us  [with_halo(): lax.ppermute(lax.slice_in_dim(block, block.shape[dim] - width, None, axis...]
    ppermute x2, starting transfers between devices: 26.5 us -> 9.37 us  [with_halo(): lax.ppermute(lax.slice_in_dim(block, block.shape[dim] - width, None, axis...]
    all_to_all x0 -> x2, starting transfers between devices: none -> 15 us  [folded_conv(): lax.all_to_all(jnp.stack([weight_rows] * lax.axis_size('member')), 'membe...]
    ppermute x2, waiting for transfers between devices: 15.1 us -> 8.24 us  [with_halo(): lax.ppermute(lax.slice_in_dim(block, 0, width, axis=dim), axis, backward)]
    all_to_all x0 -> x2, waiting for transfers between devices: none -> 4.91 us  [folded_conv(): lax.all_to_all(jnp.stack([weight_rows] * lax.axis_size('member')), 'membe...]
    psum x1, blocking collectives: 102 us -> 98.2 us  [body(): lax.psum((jnp.sum(score * area[None, :, None]), jnp.sum(area)), 'lat')]
    unnamed x24 -> x26, local copies, waits for them, and re-layouts: 6.93 us -> 10.7 us
  transfers between devices with their start and end apart: 6 -> 6, of which waited for: 4 -> 5; matrix products, arithmetic and copies ran while one was open for 4% -> 8% of each run, Pallas kernels for 0% -> 0%
where the time goes in v1:
time: 229 us; the launch traced here: 228 us
  blocking collectives  132 us (58%)
  waiting for transfers between devices  35.5 us (16%)
  starting transfers between devices  28.2 us (12%)
  local copies, waits for them, and re-layouts  15.7 us (7%)
  other arithmetic  6.91 us (3%)
  matrix products  5.22 us (2%)
  between operations  4.5 us (2%)
    psum x1, blocking collectives, body(): lax.psum((jnp.sum(score * area[None, :, None]), jnp.sum(area)), 'lat')  98.2 us
    all_gather x1, blocking collectives, body(): lax.all_gather(pred[None], 'member', axis=0, tiled=True).astype(jnp.float32)  33.7 us
    ppermute x2, waiting for transfers between devices, with_halo(): lax.ppermute(lax.slice_in_dim(block, block.shape[dim] - width, None, axis...  22.3 us
    all_to_all x2, starting transfers between devices, folded_conv(): lax.all_to_all(jnp.stack([weight_rows] * lax.axis_size('member')), 'membe...  15 us
    unnamed x26, local copies, waits for them, and re-layouts  10.7 us
    ppermute x2, starting transfers between devices, with_halo(): lax.ppermute(lax.slice_in_dim(block, block.shape[dim] - width, None, axis...  9.37 us
    ppermute x2, waiting for transfers between devices, with_halo(): lax.ppermute(lax.slice_in_dim(block, 0, width, axis=dim), axis, backward)  8.24 us
    dot_general x3, matrix products, product(): jnp.dot(left.astype(jnp.float32), right.astype(jnp.float32), precision=la...  5.1 us
  transfers between devices with their start and end apart: 6, of which 5 were waited for; matrix products, arithmetic and copies ran while one was open for 8% of the time, Pallas kernels for 0%

profile of v1, /device:TPU:1, one launch (start us, length us, event | category | flops | bytes accessed | tf_op | source)
XLA Modules:
  0.0 228.5 jit_solution(6731009335334009826)
XLA Ops:
  0.7 2.0 stack.4
  2.7 8.0 %all-to-all-start = ((bf16[16,144,256]{2,1,0:T(8,128)(2,1)}), bf16[16,144,256]{2,1,0:T(8,128)(2,1)S(1)}, u32[]{:S(2)}, u32[]{:S(2)}) async-start(bf16[16,144,256]{2,1,0:T(8,128)(2,1)} %stack.4), calls=%async_computation | async-start | bytes 2359296 | tf_op jit(solution)/shard_map/all_to_all | solution.py:40
  11.5 5.6 %collective-permute-start = (bf16[1,256,256]{2,1,0:T(8,128)(2,1)S(1)}, bf16[1,256,256]{2,1,0:T(8,128)(2,1)S(1)}, u32[]{:S(2)}, u32[]{:S(2)}) collective-permute-start(bf16[1,256,256]{2,1,0:T(8,128)(2,1)S(1)} %get-tuple-element.107), channel_id=1, source_target_pairs={{0,1},{1,2},{2,3},{3,4},{4,5},{5,6},{6,7},{7,8},{8,9},{9,10},{10,1... | collective-permute-start | bytes 393224 | tf_op jit(solution)/shard_map/ppermute | solution.py:12
  17.1 1.9 collective-permute-start.1
  19.1 11.9 %collective-permute-done = bf16[1,256,256]{2,1,0:T(8,128)(2,1)S(1)} collective-permute-done((bf16[1,256,256]{2,1,0:T(8,128)(2,1)S(1)}, bf16[1,256,256]{2,1,0:T(8,128)(2,1)S(1)}, u32[]{:S(2)}, u32[]{:S(2)}) %collective-permute-start) | collective-permute-done | bytes 131104 | tf_op jit(solution)/shard_map/ppermute | solution.py:12
  30.9 6.9 %collective-permute-done.1 = bf16[1,256,256]{2,1,0:T(8,128)(2,1)S(1)} collective-permute-done((bf16[1,256,256]{2,1,0:T(8,128)(2,1)S(1)}, bf16[1,256,256]{2,1,0:T(8,128)(2,1)S(1)}, u32[]{:S(2)}, u32[]{:S(2)}) %collective-permute-start.1) | collective-permute-done | bytes 131104 | tf_op jit(solution)/shard_map/ppermute | solution.py:15
  39.4 0.8 slice_dynamic-update-slice_fusion.4
  40.2 0.8 slice_dynamic-update-slice_fusion.3
  41.0 0.8 constant_dynamic-update-slice_fusion
  41.8 0.8 slice_dynamic-update-slice_fusion.2
  42.6 0.7 slice_dynamic-update-slice_fusion.1
  44.1 0.8 slice_dynamic-update-slice_fusion
  44.9 1.1 stack.5
  46.0 7.0 %all-to-all-start.1 = ((bf16[16,144,256]{2,1,0:T(8,128)(2,1)}), bf16[16,144,256]{2,1,0:T(8,128)(2,1)S(1)}, u32[]{:S(2)}, u32[]{:S(2)}) async-start(bf16[16,144,256]{2,1,0:T(8,128)(2,1)} %stack.5), calls=%async_computation.1 | async-start | bytes 2359296 | tf_op jit(solution)/shard_map/all_to_all | solution.py:40
  53.1 2.5 %fusion.14 = bf16[512,256]{1,0:T(8,128)(2,1)S(1)} fusion(bf16[512,2304]{1,0:T(8,128)(2,1)} %bitcast.5, bf16[2304,256]{1,0:T(8,128)(2,1)S(1)} %bitcast.51), kind=kOutput, calls=%fused_computation.24 | convolution fusion | flops 605159424 | bytes 3801088 | tf_op jit(solution)/shard_map/dot_general | solution.py:21
  55.6 3.8 %collective-permute-start.2 = (bf16[1,256,256]{2,1,0:T(8,128)(2,1)S(1)}, bf16[1,256,256]{2,1,0:T(8,128)(2,1)S(1)}, u32[]{:S(2)}, u32[]{:S(2)}) collective-permute-start(bf16[1,256,256]{2,1,0:T(8,128)(2,1)S(1)} %get-tuple-element.105), channel_id=1, source_target_pairs={{0,1},{1,2},{2,3},{3,4},{4,5},{5,6},{6,7},{7,8},{8,9},{9,10},{10,1... | collective-permute-start | bytes 393224 | tf_op jit(solution)/shard_map/ppermute | solution.py:12
  59.4 1.9 collective-permute-start.3
  62.8 10.5 %collective-permute-done.2 = bf16[1,256,256]{2,1,0:T(8,128)(2,1)S(1)} collective-permute-done((bf16[1,256,256]{2,1,0:T(8,128)(2,1)S(1)}, bf16[1,256,256]{2,1,0:T(8,128)(2,1)S(1)}, u32[]{:S(2)}, u32[]{:S(2)}) %collective-permute-start.2) | collective-permute-done | bytes 131104 | tf_op jit(solution)/shard_map/ppermute | solution.py:12
  73.2 1.4 collective-permute-done.3
  74.9 0.7 constant_dynamic-update-slice_fusion.9
  75.7 0.7 constant_dynamic-update-slice_fusion.8
  76.5 0.8 constant_dynamic-update-slice_fusion.7
  77.2 0.8 constant_dynamic-update-slice_fusion.6
  78.0 0.8 constant_dynamic-update-slice_fusion.5
  78.8 0.8 constant_dynamic-update-slice_fusion.4
  79.6 0.7 constant_dynamic-update-slice_fusion.3
  81.0 0.8 constant_dynamic-update-slice_fusion.1
  81.8 4.9 %all-to-all-done.1 = bf16[16,144,256]{2,1,0:T(8,128)(2,1)S(1)} async-done(((bf16[16,144,256]{2,1,0:T(8,128)(2,1)}), bf16[16,144,256]{2,1,0:T(8,128)(2,1)S(1)}, u32[]{:S(2)}, u32[]{:S(2)}) %all-to-all-start.1) | async-done | bytes 1179680 | tf_op jit(solution)/shard_map/all_to_all | solution.py:40
  86.7 2.4 %fusion = bf16[512,256]{1,0:T(8,128)(2,1)S(1)} fusion(bf16[512,2304]{1,0:T(8,128)(2,1)} %constant_dynamic-update-slice_fusion.1, bf16[2304,256]{1,0:T(8,128)(2,1)S(1)} %bitcast.50, bf16[512,256]{1,0:T(8,128)(2,1)S(1)} %fusion.16), kind=kOutput, calls=%fused_computation.6 | convolution fusion | flops 604372992 | bytes 4063232 | tf_op jit(solution)/shard_map/dot_general | solution.py:21
  89.3 33.7 %all_gather.3 = bf16[16,8,2,256]{3,1,2,0:T(8,128)(2,1)S(1)} all-gather(bf16[1,8,2,256]{3,1,2,0:T(8,128)(2,1)S(1)} %bitcast.60), channel_id=1, replica_groups=mesh['member'=16,'lat'=32] {'member'}, dimensions={0}, use_global_device_ids=true | all-gather | bytes 139264 | tf_op jit(solution)/shard_map/all_gather | solution.py:69
  123.1 3.4 %while.14 = (s32[]{:T(128)}, f32[8,2,256]{2,1,0:T(2,128)S(1)}, f32[16,8,2,256]{3,2,1,0:T(2,128)S(1)}, s32[]{:T(128)}, s32[]{:T(128)}) while((s32[]{:T(128)}, f32[8,2,256]{2,1,0:T(2,128)S(1)}, f32[16,8,2,256]{3,2,1,0:T(2,128)S(1)}, s32[]{:T(128)}, s32[]{:T(128)}) %tuple.48), condition=%wide.region_3.4_spmd.clone, body=%wide.region_1.3_spmd.clone.sunk | while | flops 200707 | bytes 376907 | solution.py:76
  127.9 98.2 %all-reduce.2 = (f32[]{:T(128)}, f32[]{:T(128)}) all-reduce(f32[]{:T(128)} %get-tuple-element.95, f32[]{:T(128)} %fusion.25), channel_id=1, replica_groups=mesh['member'=16,'lat'=32] {'lat'}, use_global_device_ids=true, to_apply=%region_5.6 | all-reduce | flops 2 | bytes 16 | tf_op jit(solution)/shard_map/psum | solution.py:80
  (81 shorter events, 9.0 us)
Async XLA Ops:
  0.6 10.7 %copy-start = (f32[16,256]{1,0:T(8,128)S(1)}, f32[16,256]{1,0:T(8,128)}, u32[]{:S(2)}) copy-start(f32[16,256]{1,0:T(8,128)} %param.12) | copy-start | bytes 49156
  0.6 10.8 %copy-start.1 = (bf16[1,2,256,256]{3,2,1,0:T(8,128)(2,1)S(1)}, bf16[1,2,256,256]{3,2,1,0:T(8,128)(2,1)}, u32[]{:S(2)}) copy-start(bf16[1,2,256,256]{3,2,1,0:T(8,128)(2,1)} %param.10) | copy-start | bytes 786436
  2.7 42.2 %all-to-all-start = ((bf16[16,144,256]{2,1,0:T(8,128)(2,1)}), bf16[16,144,256]{2,1,0:T(8,128)(2,1)S(1)}, u32[]{:S(2)}, u32[]{:S(2)}) async-start(bf16[16,144,256]{2,1,0:T(8,128)(2,1)} %stack.4), calls=%async_computation | async-start | bytes 2359296 | tf_op jit(solution)/shard_map/all_to_all | solution.py:40
  11.5 19.4 %collective-permute-start = (bf16[1,256,256]{2,1,0:T(8,128)(2,1)S(1)}, bf16[1,256,256]{2,1,0:T(8,128)(2,1)S(1)}, u32[]{:S(2)}, u32[]{:S(2)}) collective-permute-start(bf16[1,256,256]{2,1,0:T(8,128)(2,1)S(1)} %get-tuple-element.107), channel_id=1, source_target_pairs={{0,1},{1,2},{2,3},{3,4},{4,5},{5,6},{6,7},{7,8},{8,9},{9,10},{10,1... | collective-permute-start | bytes 393224 | tf_op jit(solution)/shard_map/ppermute | solution.py:12
  17.1 20.7 %collective-permute-start.1 = (bf16[1,256,256]{2,1,0:T(8,128)(2,1)S(1)}, bf16[1,256,256]{2,1,0:T(8,128)(2,1)S(1)}, u32[]{:S(2)}, u32[]{:S(2)}) collective-permute-start(bf16[1,256,256]{2,1,0:T(8,128)(2,1)S(1)} %get-tuple-element.108), channel_id=1, source_target_pairs={{1,0},{2,1},{3,2},{4,3},{5,4},{6,5},{7,6},{8,7},{9,8},{10,9},{11,1... | collective-permute-start | bytes 393224 | tf_op jit(solution)/shard_map/ppermute | solution.py:15
  38.7 6.2 %copy-start.2 = (bf16[144,256]{1,0:T(8,128)(2,1)S(1)}, bf16[144,256]{1,0:T(8,128)(2,1)}, u32[]{:S(2)}) copy-start(bf16[144,256]{1,0:T(8,128)(2,1)} %param.14) | copy-start | bytes 221188
  46.0 40.7 %all-to-all-start.1 = ((bf16[16,144,256]{2,1,0:T(8,128)(2,1)}), bf16[16,144,256]{2,1,0:T(8,128)(2,1)S(1)}, u32[]{:S(2)}, u32[]{:S(2)}) async-start(bf16[16,144,256]{2,1,0:T(8,128)(2,1)} %stack.5), calls=%async_computation.1 | async-start | bytes 2359296 | tf_op jit(solution)/shard_map/all_to_all | solution.py:40
  53.1 8.3 %copy-start.3 = (f32[8,2,256]{2,1,0:T(2,128)S(1)}, f32[8,2,256]{2,1,0:T(2,128)}, u32[]{:S(2)}) copy-start(f32[8,2,256]{2,1,0:T(2,128)} %param.16) | copy-start | bytes 49156
  55.6 17.6 %collective-permute-start.2 = (bf16[1,256,256]{2,1,0:T(8,128)(2,1)S(1)}, bf16[1,256,256]{2,1,0:T(8,128)(2,1)S(1)}, u32[]{:S(2)}, u32[]{:S(2)}) collective-permute-start(bf16[1,256,256]{2,1,0:T(8,128)(2,1)S(1)} %get-tuple-element.105), channel_id=1, source_target_pairs={{0,1},{1,2},{2,3},{3,4},{4,5},{5,6},{6,7},{7,8},{8,9},{9,10},{10,1... | collective-permute-start | bytes 393224 | tf_op jit(solution)/shard_map/ppermute | solution.py:12
  59.4 15.2 %collective-permute-start.3 = (bf16[1,256,256]{2,1,0:T(8,128)(2,1)S(1)}, bf16[1,256,256]{2,1,0:T(8,128)(2,1)S(1)}, u32[]{:S(2)}, u32[]{:S(2)}) collective-permute-start(bf16[1,256,256]{2,1,0:T(8,128)(2,1)S(1)} %get-tuple-element.106), channel_id=1, source_target_pairs={{1,0},{2,1},{3,2},{4,3},{5,4},{6,5},{7,6},{8,7},{9,8},{10,9},{11,1... | collective-permute-start | bytes 393224 | tf_op jit(solution)/shard_map/ppermute | solution.py:15
  81.8 7.4 %copy-start.4 = (bf16[256,8]{0,1:T(8,128)(2,1)S(1)}, bf16[256,8]{0,1:T(8,128)(2,1)}, u32[]{:S(2)}) copy-start(bf16[256,8]{0,1:T(8,128)(2,1)} %param.15) | copy-start | bytes 12292
